TPU v7x, 32 devices: a whole 2x2x4 slice. The times are simulated.
32 devices in a mesh: band: 4 (over y, x), domain: 8 (over z, core).
Axes of the slice: x: 2, y: 2, z: 4, core: 2. Of those that a mesh axis runs over, the one named last changes fastest.
Arguments:
- orbitals: float32 [6144, 512], P('domain', 'band'), may hold values from -6 to 6
- potential: float32 [6144], P('domain'), may hold values from -1 to 1
- occupation: float32 [512], P('band'), may hold values from 0 to 0.0068359375, as said below
- cell_matrix: bfloat16 [343, 343], replicated, may hold values from -1 to 2, as said below
- cell_nodes: int32 [32, 343], P('domain'), may hold values from 0 to 936, as said below
- face_order: int32 [8, 169], P('domain'), may hold values from 0 to 168, as said below
- pois_matrix: float32 [729, 729], replicated, may hold values from -1 to 2, as said below
- pois_nodes: int32 [16, 729], P('domain'), may hold values from 0 to 848, as said below
- pois_face: int32 [8, 81], P('domain'), may hold values from 0 to 80, as said below
- screening: float32 [6144], P('domain'), may hold values from 0.5 to 2
- block_owner: int32 [8, 8], P('domain'), may hold values from 0 to 7, as said below
Outputs:
- filtered: float32 [6144, 512], P('domain', 'band')
- hartree: float32 [6144], P('domain')
Inputs may be any that keep to these rules, and one draw needn't show every extreme that they name: `occupation`: positive weights. `cell_matrix`: symmetric. `pois_matrix`: symmetric. `cell_nodes`: cell c (counted from 0 within its domain) uses the local nodes (c * 234 + k) mod 937 for k < 343, in a drawn order. `pois_nodes`: cell c (counted from 0 within its domain) uses the local nodes (c * 424 + k) mod 849 for k < 729, in a drawn order. `face_order`: each row is a permutation. `pois_face`: each row is a permutation. `block_owner`: each row is a permutation.
All inputs are finite; a program needn't handle non-finite values.
Results may differ from a plain program's by a relative error of at most 0.0065.
The roundings to bfloat16 on the way count: a program that leaves them out, or rounds other values in their place, can miss the bound.
Values may be sent and summed in bfloat16 or wider, within the bound.
No kernel may reach another device: no remote copies, remote signals or barrier semaphores. Data moves between devices by JAX's collectives and lax.ppermute only.
A program may use at most 64 MiB of HBM per device.

v0:
```python
import jax
import jax.numpy as jnp
from jax import lax
from jax.sharding import PartitionSpec as P

filter_center = 1.8
filter_half = 2.7
solve_center = 3.25
solve_half = 2.75
solve_ratio = solve_center / solve_half
weight_zero = 1.0 / solve_ratio
weight_one = 1.0 / (2.0 * solve_ratio - weight_zero)
weight_two = 1.0 / (2.0 * solve_ratio - weight_one)


def from_behind(array, axis, by):
    length = lax.axis_size(axis)
    return lax.ppermute(array, axis, [(i, (i + by) % length) for i in range(length)])


def filter_step(applied, current, earlier):
    if earlier is None:
        return (applied - filter_center * current) / filter_half
    return 2.0 * (applied - filter_center * current) / filter_half - earlier


def next_rows(values, face_row):
    coming = from_behind(values, "domain", -1)
    return jnp.take(coming, face_row, axis=0)


def next_low_rows(values, face_row):
    coming = from_behind(values, "domain", -1)
    return jnp.take(coming, face_row, axis=0)


def fold_back(upper_rows, face_row):
    ordered = jnp.zeros_like(upper_rows).at[face_row].set(upper_rows)
    return from_behind(ordered, "domain", 1)


def assembled(owned_rows, face_row, terms):
    owned_count = owned_rows.shape[0]
    shared = face_row.shape[0]
    local_rows = jnp.concatenate([owned_rows, next_rows(owned_rows[:shared], face_row)], axis=0)
    partial_value = terms(local_rows)
    arrived = fold_back(partial_value[owned_count:], face_row)
    return partial_value[:owned_count].at[:shared].add(arrived)


def assembled_low(owned_rows, face_row, terms):
    owned_count = owned_rows.shape[0]
    shared = face_row.shape[0]
    low_rows = owned_rows.astype(jnp.bfloat16)
    local_rows = jnp.concatenate([low_rows, next_low_rows(low_rows[:shared], face_row)], axis=0)
    partial_value = terms(local_rows)
    arrived = fold_back(partial_value[owned_count:], face_row)
    return partial_value[:owned_count].at[:shared].add(arrived)


def cell_terms(local_rows, cell_matrix, node_ids):
    cell_vals = jnp.take(local_rows, node_ids, axis=0)
    product = jnp.einsum("pq,cqm->cpm", cell_matrix, cell_vals, preferred_element_type=jnp.float32)
    columns = local_rows.shape[1]
    return (
        jnp.zeros(local_rows.shape, jnp.float32)
        .at[node_ids.reshape(-1)]
        .add(product.reshape(-1, columns))
    )


def field_terms(local_rows, pois_matrix, node_ids):
    cell_vals = jnp.take(local_rows, node_ids, axis=0)
    product = jnp.einsum(
        "pq,cq->cp",
        pois_matrix,
        cell_vals,
        precision=lax.Precision.HIGHEST,
        preferred_element_type=jnp.float32,
    )
    return (
        jnp.zeros(local_rows.shape, jnp.float32).at[node_ids.reshape(-1)].add(product.reshape(-1))
    )


def reshuffle(blocks):
    return lax.all_to_all(blocks, "domain", split_axis=0, concat_axis=0, tiled=True)


def band_total(values):
    return lax.psum(values, "band")


def per_device(
    orbitals,
    potential,
    occupation,
    cell_matrix,
    cell_nodes,
    face_order,
    pois_matrix,
    pois_nodes,
    pois_face,
    screening,
    block_owner,
):
    domains = lax.axis_size("domain")
    owned_count = orbitals.shape[0]
    block_len = owned_count // domains
    face_row = face_order[0]
    owner_row = block_owner[0]
    field_face = pois_face[0]

    def orbital_terms(local_rows):
        return cell_terms(local_rows, cell_matrix, cell_nodes)

    def hamiltonian(vector, potential_in):
        return assembled_low(vector, face_row, orbital_terms) + potential_in[:, None] * vector

    filter_one = filter_step(hamiltonian(orbitals, potential), orbitals, None)
    filter_two = filter_step(hamiltonian(filter_one, potential), filter_one, orbitals)
    filter_three = filter_step(hamiltonian(filter_two, potential), filter_two, filter_one)
    partial_value = jnp.dot(
        filter_three * filter_three,
        occupation,
        precision=lax.Precision.HIGHEST,
        preferred_element_type=jnp.float32,
    )
    summed = band_total(partial_value)
    arranged = (
        jnp.zeros((domains, block_len), jnp.float32)
        .at[owner_row]
        .set(summed.reshape(domains, block_len))
    )
    source = reshuffle(arranged).reshape(owned_count)

    def field_operator(vector):
        return (
            assembled(
                vector,
                field_face,
                lambda local_rows: field_terms(local_rows, pois_matrix, pois_nodes),
            )
            + screening * vector
        )

    step_one = source / solve_center
    residual = source - field_operator(step_one)
    step_two = weight_one * weight_zero * step_one + 2.0 * weight_one / solve_half * residual
    residual = residual - field_operator(step_two)
    step_three = weight_two * weight_one * step_two + 2.0 * weight_two / solve_half * residual
    solution = step_one + step_two + step_three
    returned = reshuffle(solution.reshape(domains, block_len))
    hartree = jnp.take(returned, owner_row, axis=0).reshape(owned_count)
    potential_new = potential + hartree
    refilter_one = filter_step(hamiltonian(filter_three, potential_new), filter_three, None)
    refilter_two = filter_step(hamiltonian(refilter_one, potential_new), refilter_one, filter_three)
    return (refilter_two, hartree)


def solution(mesh):
    return jax.shard_map(
        per_device,
        mesh=mesh,
        in_specs=(
            P("domain", "band"),
            P("domain"),
            P("band"),
            P(),
            P("domain", None),
            P("domain", None),
            P(),
            P("domain", None),
            P("domain", None),
            P("domain"),
            P("domain", None),
        ),
        out_specs=(P("domain", "band"), P("domain")),
        check_vma=False,
    )
```

profile of v0, /device:TPU:0, one launch (start us, length us, event | category | flops | bytes accessed | tf_op | source)
XLA Modules:
  0.0 261.4 jit_solution(17496827061707327766)
XLA Ops:
  1.8 4.6 %collective-permute-start = (bf16[169,128]{1,0:T(8,128)(2,1)S(1)}, bf16[169,128]{1,0:T(8,128)(2,1)S(1)}, u32[]{:S(2)}, u32[]{:S(2)}) collective-permute-start(bf16[169,128]{1,0:T(8,128)(2,1)S(1)} %slice.251), channel_id=1, source_target_pairs={{0,7},{1,0},{2,1},{3,2},{4,3},{5,4},{6,5},{7,6},{8,15},{9,8},{10,9... | collective-permute-start | bytes 129800 | tf_op jit(solution)/shard_map/ppermute | solution.py:18
  13.0 3.3 %gather_fusion.2 = bf16[1372,128]{1,0:T(8,128)(2,1)S(1)} fusion(bf16[937,128]{1,0:T(8,128)(2,1)S(1)} %pad_maximum_fusion, s32[2048]{0:T(1024)S(1)} %pad_clamp_fusion.1), kind=kCustom, calls=%fused_computation.1.clone | custom fusion | bytes 707952 | tf_op jit(solution)/shard_map/jit(_take)/gather | solution.py:62
  19.9 9.9 %scatter_custom_fusion = f32[937,128]{1,0:T(8,128)} fusion(s32[1372]{0:T(1024)S(1)} %fusion.51, f32[1372,128]{1,0:T(8,128)} %reshape.513, f32[]{:T(128)} %constant.233.clone.1), kind=kCustom, calls=%fused_computation.72 | custom fusion | flops 175616 | bytes 480256 | tf_op jit(solution)/shard_map/scatter-add | solution.py:68
  32.8 4.1 %collective-permute-done.1 = f32[169,128]{1,0:T(8,128)S(1)} collective-permute-done((f32[169,128]{1,0:T(8,128)S(1)}, f32[169,128]{1,0:T(8,128)S(1)}, u32[]{:S(2)}, u32[]{:S(2)}) %collective-permute-start.1) | collective-permute-done | bytes 86560 | tf_op jit(solution)/shard_map/ppermute | solution.py:18
  43.7 4.4 %gather_fusion.4 = bf16[1372,128]{1,0:T(8,128)(2,1)} fusion(bf16[937,128]{1,0:T(8,128)(2,1)S(1)} %pad_maximum_fusion.1, s32[2048]{0:T(1024)} %copy-done.7), kind=kCustom, calls=%fused_computation.8.clone | custom fusion | bytes 707952 | tf_op jit(solution)/shard_map/jit(_take)/gather | solution.py:62
  49.9 2.4 convolution_bitcast_fusion.3
  52.4 2.1 reshape.529
  54.4 9.9 %scatter_custom_fusion.2 = f32[937,128]{1,0:T(8,128)} fusion(s32[1372]{0:T(1024)} %copy-done.25, f32[1372,128]{1,0:T(8,128)} %reshape.529, f32[]{:T(128)} %constant.233.clone.1), kind=kCustom, calls=%fused_computation.70 | custom fusion | flops 175616 | bytes 480256 | tf_op jit(solution)/shard_map/scatter-add | solution.py:68
  68.1 3.4 %collective-permute-done.3 = f32[169,128]{1,0:T(8,128)S(1)} collective-permute-done((f32[169,128]{1,0:T(8,128)S(1)}, f32[169,128]{1,0:T(8,128)S(1)}, u32[]{:S(2)}, u32[]{:S(2)}) %collective-permute-start.3) | collective-permute-done | bytes 86560 | tf_op jit(solution)/shard_map/ppermute | solution.py:18
  79.1 4.0 %gather_fusion.6 = bf16[1372,128]{1,0:T(8,128)(2,1)} fusion(bf16[937,128]{1,0:T(8,128)(2,1)S(1)} %pad_maximum_fusion.2, s32[2048]{0:T(1024)S(1)} %copy-done.8), kind=kCustom, calls=%fused_computation.9.clone | custom fusion | bytes 707952 | tf_op jit(solution)/shard_map/jit(_take)/gather | solution.py:62
  87.6 9.9 %scatter_custom_fusion.4 = f32[937,128]{1,0:T(8,128)} fusion(s32[1372]{0:T(1024)} %copy-done.25, f32[1372,128]{1,0:T(8,128)} %reshape.545, f32[]{:T(128)} %constant.233.clone.1), kind=kCustom, calls=%fused_computation.68 | custom fusion | flops 175616 | bytes 480256 | tf_op jit(solution)/shard_map/scatter-add | solution.py:68
  100.7 4.0 %collective-permute-done.5 = f32[169,128]{1,0:T(8,128)S(1)} collective-permute-done((f32[169,128]{1,0:T(8,128)S(1)}, f32[169,128]{1,0:T(8,128)S(1)}, u32[]{:S(2)}, u32[]{:S(2)}) %collective-permute-start.5) | collective-permute-done | bytes 86560 | tf_op jit(solution)/shard_map/ppermute | solution.py:18
  109.9 9.9 %psum.7 = f32[8,96]{1,0:T(8,128)S(1)} all-reduce(f32[8,96]{1,0:T(8,128)S(1)} %reshape.383), channel_id=1, replica_groups=mesh['band'=4,'domain'=8] {'band'}, use_global_device_ids=true, to_apply=%region_8.11 | all-reduce | flops 768 | bytes 6144 | tf_op jit(solution)/shard_map/psum | solution.py:91
  121.1 3.3 %all-to-all-start = ((f32[8,1,96]{2,1,0:T(1,128)}), f32[8,1,96]{2,1,0:T(1,128)S(1)}, u32[]{:S(2)}, u32[]{:S(2)}) async-start(f32[8,1,96]{2,1,0:T(1,128)} %bitcast.12), calls=%async_computation | async-start | bytes 8192 | tf_op jit(solution)/shard_map/all_to_all | solution.py:87
  124.4 5.4 %all-to-all-done = f32[8,1,96]{2,1,0:T(1,128)S(1)} async-done(((f32[8,1,96]{2,1,0:T(1,128)}), f32[8,1,96]{2,1,0:T(1,128)S(1)}, u32[]{:S(2)}, u32[]{:S(2)}) %all-to-all-start) | async-done | bytes 3104 | tf_op jit(solution)/shard_map/all_to_all | solution.py:87
  134.3 5.6 %gather_fusion.10 = f32[1458]{0:T(1024)S(1)} fusion(f32[849]{0:T(1024)S(1)} %pad_maximum_fusion.5, s32[2048]{0:T(1024)S(1)} %pad_clamp_fusion), kind=kCustom, calls=%fused_computation.3.clone | custom fusion | bytes 17496 | tf_op jit(solution)/shard_map/jit(_take)/gather | solution.py:73
  142.2 11.0 %scatter_custom_fusion.9 = f32[849]{0:T(1024)S(1)} fusion(s32[1458]{0:T(1024)S(1)} %fusion.46, f32[1458]{0:T(1024)S(1)} %reshape.585, f32[]{:T(128)} %constant.233.clone.1), kind=kCustom, calls=%fused_computation.137 | custom fusion | flops 1458 | bytes 3400 | tf_op jit(solution)/shard_map/scatter-add | solution.py:82
  155.7 3.3 %collective-permute-done.9 = f32[81]{0:T(128)S(1)} collective-permute-done((f32[81]{0:T(128)S(1)}, f32[81]{0:T(128)S(1)}, u32[]{:S(2)}, u32[]{:S(2)}) %collective-permute-start.9) | collective-permute-done | bytes 356 | tf_op jit(solution)/shard_map/ppermute | solution.py:18
  161.9 5.7 %gather_fusion.12 = f32[1458]{0:T(1024)S(1)} fusion(f32[849]{0:T(1024)S(1)} %pad_maximum_fusion.6, s32[2048]{0:T(1024)S(1)} %pad_clamp_fusion), kind=kCustom, calls=%fused_computation.13.clone | custom fusion | bytes 17496 | tf_op jit(solution)/shard_map/jit(_take)/gather | solution.py:73
  169.7 11.0 %scatter_custom_fusion.11 = f32[849]{0:T(1024)S(1)} fusion(s32[1458]{0:T(1024)S(1)} %fusion.46, f32[1458]{0:T(1024)S(1)} %reshape.601, f32[]{:T(128)} %constant.233.clone.1), kind=kCustom, calls=%fused_computation.135 | custom fusion | flops 1458 | bytes 3400 | tf_op jit(solution)/shard_map/scatter-add | solution.py:82
  181.8 4.7 %collective-permute-done.11 = f32[81]{0:T(128)S(1)} collective-permute-done((f32[81]{0:T(128)S(1)}, f32[81]{0:T(128)S(1)}, u32[]{:S(2)}, u32[]{:S(2)}) %collective-permute-start.11) | collective-permute-done | bytes 356 | tf_op jit(solution)/shard_map/ppermute | solution.py:18
  187.3 3.3 %all-to-all-start.1 = ((f32[8,1,96]{2,1,0:T(1,128)}), f32[8,1,96]{2,1,0:T(1,128)S(1)}, u32[]{:S(2)}, u32[]{:S(2)}) async-start(f32[8,1,96]{2,1,0:T(1,128)} %all_to_all.16), calls=%async_computation.1 | async-start | bytes 8192 | tf_op jit(solution)/shard_map/all_to_all | solution.py:87
  190.6 3.5 %collective-permute-start.6 = (bf16[169,128]{1,0:T(8,128)(2,1)S(1)}, bf16[169,128]{1,0:T(8,128)(2,1)S(1)}, u32[]{:S(2)}, u32[]{:S(2)}) collective-permute-start(bf16[169,128]{1,0:T(8,128)(2,1)S(1)} %slice.263), channel_id=1, source_target_pairs={{0,7},{1,0},{2,1},{3,2},{4,3},{5,4},{6,5},{7,6},{8,15},{9,8},{10,9... | collective-permute-start | bytes 129800 | tf_op jit(solution)/shard_map/ppermute | solution.py:18
  197.6 4.0 %gather_fusion.8 = bf16[1372,128]{1,0:T(8,128)(2,1)} fusion(bf16[937,128]{1,0:T(8,128)(2,1)S(1)} %pad_maximum_fusion.3, s32[2048]{0:T(1024)S(1)} %copy-done.8), kind=kCustom, calls=%fused_computation.10.clone | custom fusion | bytes 707952 | tf_op jit(solution)/shard_map/jit(_take)/gather | solution.py:62
  204.2 2.0 reshape.561
  206.2 9.3 %scatter_custom_fusion.6 = f32[937,128]{1,0:T(8,128)S(1)} fusion(s32[1372]{0:T(1024)} %copy-done.25, f32[1372,128]{1,0:T(8,128)} %reshape.561, f32[]{:T(128)} %constant.233.clone.1), kind=kCustom, calls=%fused_computation.66 | custom fusion | flops 175616 | bytes 480256 | tf_op jit(solution)/shard_map/scatter-add | solution.py:68
  218.8 4.3 %collective-permute-done.7 = f32[169,128]{1,0:T(8,128)S(1)} collective-permute-done((f32[169,128]{1,0:T(8,128)}, f32[169,128]{1,0:T(8,128)S(1)}, u32[]{:S(2)}, u32[]{:S(2)}) %collective-permute-start.7) | collective-permute-done | bytes 86560 | tf_op jit(solution)/shard_map/ppermute | solution.py:18
  229.2 4.4 %gather_fusion.14 = bf16[1372,128]{1,0:T(8,128)(2,1)} fusion(bf16[937,128]{1,0:T(8,128)(2,1)S(1)} %pad_maximum_fusion.4, s32[2048]{0:T(1024)} %copy-done.7), kind=kCustom, calls=%fused_computation.11.clone | custom fusion | bytes 707952 | tf_op jit(solution)/shard_map/jit(_take)/gather | solution.py:62
  235.4 2.4 convolution_bitcast_fusion
  239.7 9.9 %scatter_custom_fusion.13 = f32[937,128]{1,0:T(8,128)} fusion(s32[1372]{0:T(1024)} %copy-done.25, f32[1372,128]{1,0:T(8,128)} %reshape.617, f32[]{:T(128)} %constant.233.clone.1), kind=kCustom, calls=%fused_computation.64 | custom fusion | flops 175616 | bytes 480256 | tf_op jit(solution)/shard_map/scatter-add | solution.py:68
  252.8 4.0 %collective-permute-done.13 = f32[169,128]{1,0:T(8,128)S(1)} collective-permute-done((f32[169,128]{1,0:T(8,128)S(1)}, f32[169,128]{1,0:T(8,128)S(1)}, u32[]{:S(2)}, u32[]{:S(2)}) %collective-permute-start.13) | collective-permute-done | bytes 86560 | tf_op jit(solution)/shard_map/ppermute | solution.py:18
  259.4 2.0 multiply_subtract_fusion
  (198 shorter events, 88.9 us)
Async XLA Ops:
  0.6 139.5 %copy-start = (f32[729,729]{1,0:T(8,128)S(1)}, f32[729,729]{1,0:T(8,128)}, u32[]{:S(2)}) copy-start(f32[729,729]{1,0:T(8,128)} %param.39) | copy-start | bytes 6377296
  1.8 10.3 %collective-permute-start = (bf16[169,128]{1,0:T(8,128)(2,1)S(1)}, bf16[169,128]{1,0:T(8,128)(2,1)S(1)}, u32[]{:S(2)}, u32[]{:S(2)}) collective-permute-start(bf16[169,128]{1,0:T(8,128)(2,1)S(1)} %slice.251), channel_id=1, source_target_pairs={{0,7},{1,0},{2,1},{3,2},{4,3},{5,4},{6,5},{7,6},{8,15},{9,8},{10,9... | collective-permute-start | bytes 129800 | tf_op jit(solution)/shard_map/ppermute | solution.py:18
  16.5 22.1 %copy-start.2 = (f32[768,128]{1,0:T(8,128)S(1)}, f32[768,128]{1,0:T(8,128)}, u32[]{:S(2)}) copy-start(f32[768,128]{1,0:T(8,128)} %param.33) | copy-start | bytes 1179652
  31.1 5.8 %collective-permute-start.1 = (f32[169,128]{1,0:T(8,128)S(1)}, f32[169,128]{1,0:T(8,128)S(1)}, u32[]{:S(2)}, u32[]{:S(2)}) collective-permute-start(f32[169,128]{1,0:T(8,128)S(1)} %scatter_custom_fusion.1), channel_id=1, source_target_pairs={{0,1},{1,2},{2,3},{3,4},{4,5},{5,6},{6,7},{7,0},{8,9},{9,10},{10,1... | collective-permute-start | bytes 259592 | tf_op jit(solution)/shard_map/ppermute | solution.py:18
  39.5 1.8 collective-permute-start.2
  49.9 24.1 %copy-start.4 = (f32[768,128]{1,0:T(8,128)S(1)}, f32[768,128]{1,0:T(8,128)}, u32[]{:S(2)}) copy-start(f32[768,128]{1,0:T(8,128)} %copy-done.3) | copy-start | bytes 1179652
  49.9 24.1 %copy-start.10 = (f32[768]{0:T(1024)S(1)}, f32[768]{0:T(1024)}, u32[]{:S(2)}) copy-start(f32[768]{0:T(1024)} %param.34) | copy-start | bytes 9220
  49.9 24.1 %copy-start.14 = (f32[768]{0:T(1024)S(1)}, f32[768]{0:T(1024)}, u32[]{:S(2)}) copy-start(f32[768]{0:T(1024)} %broadcast_multiply_fusion.2) | copy-start | bytes 9220
  52.4 23.4 %copy-start.30 = (s32[1,8]{1,0:T(1,128)S(1)}, s32[1,8]{1,0:T(1,128)}, u32[]{:S(2)}) copy-start(s32[1,8]{1,0:T(1,128)} %param.43) | copy-start | bytes 100
  52.4 23.9 %copy-start.11 = (s32[2,729]{1,0:T(2,128)S(1)}, s32[2,729]{1,0:T(2,128)}, u32[]{:S(2)}) copy-start(s32[2,729]{1,0:T(2,128)} %param.40) | copy-start | bytes 17500
  52.4 24.0 %copy-start.17 = (s32[2,729]{1,0:T(2,128)S(1)}, s32[2,729]{1,0:T(2,128)}, u32[]{:S(2)}) copy-start(s32[2,729]{1,0:T(2,128)} %compare_select_fusion.2) | copy-start | bytes 17500
  54.4 24.6 %copy-start.8 = (s32[2048]{0:T(1024)S(1)}, s32[2048]{0:T(1024)}, u32[]{:S(2)}) copy-start(s32[2048]{0:T(1024)} %copy-done.7) | copy-start | bytes 24580
  65.7 5.8 %collective-permute-start.3 = (f32[169,128]{1,0:T(8,128)S(1)}, f32[169,128]{1,0:T(8,128)S(1)}, u32[]{:S(2)}, u32[]{:S(2)}) collective-permute-start(f32[169,128]{1,0:T(8,128)S(1)} %scatter_custom_fusion.3), channel_id=1, source_target_pairs={{0,1},{1,2},{2,3},{3,4},{4,5},{5,6},{6,7},{7,0},{8,9},{9,10},{10,1... | collective-permute-start | bytes 259592 | tf_op jit(solution)/shard_map/ppermute | solution.py:18
  75.3 2.1 collective-permute-start.4
  98.8 5.8 %collective-permute-start.5 = (f32[169,128]{1,0:T(8,128)S(1)}, f32[169,128]{1,0:T(8,128)S(1)}, u32[]{:S(2)}, u32[]{:S(2)}) collective-permute-start(f32[169,128]{1,0:T(8,128)S(1)} %scatter_custom_fusion.5), channel_id=1, source_target_pairs={{0,1},{1,2},{2,3},{3,4},{4,5},{5,6},{6,7},{7,0},{8,9},{9,10},{10,1... | collective-permute-start | bytes 259592 | tf_op jit(solution)/shard_map/ppermute | solution.py:18
  121.1 8.8 %all-to-all-start = ((f32[8,1,96]{2,1,0:T(1,128)}), f32[8,1,96]{2,1,0:T(1,128)S(1)}, u32[]{:S(2)}, u32[]{:S(2)}) async-start(f32[8,1,96]{2,1,0:T(1,128)} %bitcast.12), calls=%async_computation | async-start | bytes 8192 | tf_op jit(solution)/shard_map/all_to_all | solution.py:87
  131.1 1.3 collective-permute-start.8
  140.0 21.8 %copy-start.29 = (s32[1,81]{1,0:T(1,128)S(1)}, s32[1,81]{1,0:T(1,128)}, u32[]{:S(2)}) copy-start(s32[1,81]{1,0:T(1,128)} %param.41) | copy-start | bytes 976
  154.2 4.8 %collective-permute-start.9 = (f32[81]{0:T(128)S(1)}, f32[81]{0:T(128)S(1)}, u32[]{:S(2)}, u32[]{:S(2)}) collective-permute-start(f32[81]{0:T(128)S(1)} %scatter_custom_fusion.10), channel_id=1, source_target_pairs={{0,1},{1,2},{2,3},{3,4},{4,5},{5,6},{6,7},{7,0},{8,9},{9,10},{10,1... | collective-permute-start | bytes 980 | tf_op jit(solution)/shard_map/ppermute | solution.py:18
  159.0 1.6 collective-permute-start.10
  167.6 23.0 %copy-start.27 = (s32[8]{0:T(128)S(1)}, s32[8]{0:T(128)}, u32[]{:S(2)}) copy-start(s32[8]{0:T(128)} %fusion.60) | copy-start | bytes 100
  167.6 29.2 %copy-start.19 = (s32[1024]{0:T(1024)S(1)}, s32[1024]{0:T(1024)}, u32[]{:S(2)}) copy-start(s32[1024]{0:T(1024)} %copy-done.18) | copy-start | bytes 12292
  167.6 29.9 %copy-start.24 = (pred[169]{0:T(512)(128)(4,1)S(1)}, pred[169]{0:T(512)(128)(4,1)}, u32[]{:S(2)}) copy-start(pred[169]{0:T(512)(128)(4,1)} %copy-done.23) | copy-start | bytes 511
  181.7 4.8 %collective-permute-start.11 = (f32[81]{0:T(128)S(1)}, f32[81]{0:T(128)S(1)}, u32[]{:S(2)}, u32[]{:S(2)}) collective-permute-start(f32[81]{0:T(128)S(1)} %scatter_custom_fusion.12), channel_id=1, source_target_pairs={{0,1},{1,2},{2,3},{3,4},{4,5},{5,6},{6,7},{7,0},{8,9},{9,10},{10,1... | collective-permute-start | bytes 980 | tf_op jit(solution)/shard_map/ppermute | solution.py:18
  187.3 8.8 %all-to-all-start.1 = ((f32[8,1,96]{2,1,0:T(1,128)}), f32[8,1,96]{2,1,0:T(1,128)S(1)}, u32[]{:S(2)}, u32[]{:S(2)}) async-start(f32[8,1,96]{2,1,0:T(1,128)} %all_to_all.16), calls=%async_computation.1 | async-start | bytes 8192 | tf_op jit(solution)/shard_map/all_to_all | solution.py:87
  190.6 6.1 %collective-permute-start.6 = (bf16[169,128]{1,0:T(8,128)(2,1)S(1)}, bf16[169,128]{1,0:T(8,128)(2,1)S(1)}, u32[]{:S(2)}, u32[]{:S(2)}) collective-permute-start(bf16[169,128]{1,0:T(8,128)(2,1)S(1)} %slice.263), channel_id=1, source_target_pairs={{0,7},{1,0},{2,1},{3,2},{4,3},{5,4},{6,5},{7,6},{8,15},{9,8},{10,9... | collective-permute-start | bytes 129800 | tf_op jit(solution)/shard_map/ppermute | solution.py:18
  196.7 20.4 %copy-start.22 = (f32[768]{0:T(1024)}, f32[768]{0:T(1024)S(1)}, u32[]{:S(2)}) copy-start(f32[768]{0:T(1024)S(1)} %select_n.110) | copy-start | bytes 9220
  217.2 6.0 %collective-permute-start.7 = (f32[169,128]{1,0:T(8,128)}, f32[169,128]{1,0:T(8,128)S(1)}, u32[]{:S(2)}, u32[]{:S(2)}) collective-permute-start(f32[169,128]{1,0:T(8,128)} %scatter_custom_fusion.7), channel_id=1, source_target_pairs={{0,1},{1,2},{2,3},{3,4},{4,5},{5,6},{6,7},{7,0},{8,9},{9,10},{10,1... | collective-permute-start | bytes 259592 | tf_op jit(solution)/shard_map/ppermute | solution.py:18
  225.6 1.7 collective-permute-start.12
  235.4 24.0 %copy-start.16 = (f32[768]{0:T(1024)S(1)}, f32[768]{0:T(1024)}, u32[]{:S(2)}) copy-start(f32[768]{0:T(1024)} %copy-done.15) | copy-start | bytes 9220
  235.4 24.0 %copy-start.20 = (f32[768]{0:T(1024)S(1)}, f32[768]{0:T(1024)}, u32[]{:S(2)}) copy-start(f32[768]{0:T(1024)} %get-tuple-element.90) | copy-start | bytes 9220
  251.0 5.8 %collective-permute-start.13 = (f32[169,128]{1,0:T(8,128)S(1)}, f32[169,128]{1,0:T(8,128)S(1)}, u32[]{:S(2)}, u32[]{:S(2)}) collective-permute-start(f32[169,128]{1,0:T(8,128)S(1)} %scatter_custom_fusion.14), channel_id=1, source_target_pairs={{0,1},{1,2},{2,3},{3,4},{4,5},{5,6},{6,7},{7,0},{8,9},{9,10},{10,1... | collective-permute-start | bytes 259592 | tf_op jit(solution)/shard_map/ppermute | solution.py:18
  (16 other events, 143.1 us)
where the time goes:
time: 263 us; the launch traced here: 261 us
  other arithmetic  95.7 us (36%)
  local copies, waits for them, and re-layouts  82.8 us (31%)
  waiting for transfers between devices  40.4 us (15%)
  starting transfers between devices  17.3 us (7%)
  matrix products  13.9 us (5%)
  blocking collectives  9.88 us (4%)
    scatter-add x5, other arithmetic, cell_terms(): return jnp.zeros(local_rows.shape, jnp.float32).at[node_ids.reshape(-1)]....  48.8 us
    ppermute x14, waiting for transfers between devices, from_behind(): lax.ppermute(array, axis, [(i, (i + by) % length) for i in range(length)])  33 us
    gather x10, local copies, waits for them, and re-layouts, cell_terms(): cell_vals = jnp.take(local_rows, node_ids, axis=0)  26.1 us
    scatter-add x2, other arithmetic, field_terms(): jnp.zeros(local_rows.shape, jnp.float32).at[node_ids.reshape(-1)]  22.1 us
    gather x4, local copies, waits for them, and re-layouts, field_terms(): cell_vals = jnp.take(local_rows, node_ids, axis=0)  11.5 us
    ppermute x14, starting transfers between devices, from_behind(): lax.ppermute(array, axis, [(i, (i + by) % length) for i in range(length)])  10.7 us
    reshape x5, local copies, waits for them, and re-layouts, cell_terms(): product.reshape(-1, columns)  10.1 us
    psum x1, blocking collectives, band_total(): return lax.psum(values, 'band')  9.88 us
  transfers between devices with their start and end apart: 16, of which 14 were waited for; matrix products, arithmetic and copies ran while one was open for 7% of the time, Pallas kernels for 0%

commit v1 on v0

--- a/solution.py
+++ b/solution.py
@@ -1,3 +1,4 @@
+import functools
 import jax
 import jax.numpy as jnp
 from jax import lax
@@ -11,6 +12,13 @@
 weight_zero = 1.0 / solve_ratio
 weight_one = 1.0 / (2.0 * solve_ratio - weight_zero)
 weight_two = 1.0 / (2.0 * solve_ratio - weight_one)
+
+
+def advance_the_teams(obj, device_axis):
+    return jnp.sum(lax.all_gather(obj, device_axis), 0)
+
+
+launch_case = functools.partial(advance_the_teams, device_axis="band")
 
 
 def from_behind(array, axis, by):
@@ -88,7 +96,7 @@
 
 
 def band_total(values):
-    return lax.psum(values, "band")
+    return launch_case(values)
 
 
 def per_device(

time: 263 us -> 262 us (level)
    psum x1 -> x0, blocking collectives: 9.88 us -> none  [band_total(): return lax.psum(values, 'band')]
    all_gather x0 -> x1, blocking collectives: none -> 8.2 us  [advance_the_teams(): return jnp.sum(lax.all_gather(obj, device_axis), 0)]
where the time goes in v1:
time: 262 us; the launch traced here: 260 us
  other arithmetic  95.9 us (37%)
  local copies, waits for them, and re-layouts  82.8 us (32%)
  waiting for transfers between devices  40.2 us (15%)
  starting transfers between devices  17.3 us (7%)
  matrix products  13.9 us (5%)
  blocking collectives  8.2 us (3%)
    scatter-add x5, other arithmetic, cell_terms(): return jnp.zeros(local_rows.shape, jnp.float32).at[node_ids.reshape(-1)]....  48.9 us
    ppermute x14, waiting for transfers between devices, from_behind(): lax.ppermute(array, axis, [(i, (i + by) % length) for i in range(length)])  32.9 us
    gather x10, local copies, waits for them, and re-layouts, cell_terms(): cell_vals = jnp.take(local_rows, node_ids, axis=0)  26 us
    scatter-add x2, other arithmetic, field_terms(): jnp.zeros(local_rows.shape, jnp.float32).at[node_ids.reshape(-1)]  22.1 us
    gather x4, local copies, waits for them, and re-layouts, field_terms(): cell_vals = jnp.take(local_rows, node_ids, axis=0)  11.5 us
    ppermute x14, starting transfers between devices, from_behind(): lax.ppermute(array, axis, [(i, (i + by) % length) for i in range(length)])  10.7 us
    reshape x5, local copies, waits for them, and re-layouts, cell_terms(): product.reshape(-1, columns)  10.1 us
    dot_general x5, matrix products, cell_terms(): jnp.einsum('pq,cqm->cpm', cell_matrix, cell_vals, preferred_element_type=...  8.97 us
  transfers between devices with their start and end apart: 16, of which 14 were waited for; matrix products, arithmetic and copies ran while one was open for 7% of the time, Pallas kernels for 0%

profile of v1, /device:TPU:0, one launch (start us, length us, event | category | flops | bytes accessed | tf_op | source)
XLA Modules:
  0.0 259.7 jit_solution(16906665983128226566)
XLA Ops:
  1.8 4.6 %collective-permute-start = (bf16[169,128]{1,0:T(8,128)(2,1)S(1)}, bf16[169,128]{1,0:T(8,128)(2,1)S(1)}, u32[]{:S(2)}, u32[]{:S(2)}) collective-permute-start(bf16[169,128]{1,0:T(8,128)(2,1)S(1)} %slice.251), channel_id=1, source_target_pairs={{0,7},{1,0},{2,1},{3,2},{4,3},{5,4},{6,5},{7,6},{8,15},{9,8},{10,9... | collective-permute-start | bytes 129800 | tf_op jit(solution)/shard_map/ppermute | solution.py:26
  13.0 3.3 %gather_fusion.2 = bf16[1372,128]{1,0:T(8,128)(2,1)S(1)} fusion(bf16[937,128]{1,0:T(8,128)(2,1)S(1)} %pad_maximum_fusion, s32[2048]{0:T(1024)S(1)} %pad_clamp_fusion.1), kind=kCustom, calls=%fused_computation.1.clone | custom fusion | bytes 707952 | tf_op jit(solution)/shard_map/jit(_take)/gather | solution.py:70
  19.9 9.9 %scatter_custom_fusion = f32[937,128]{1,0:T(8,128)} fusion(s32[1372]{0:T(1024)S(1)} %fusion.51, f32[1372,128]{1,0:T(8,128)} %reshape.513, f32[]{:T(128)} %constant.234.clone.1), kind=kCustom, calls=%fused_computation.72 | custom fusion | flops 175616 | bytes 480256 | tf_op jit(solution)/shard_map/scatter-add | solution.py:76
  32.8 4.1 %collective-permute-done.1 = f32[169,128]{1,0:T(8,128)S(1)} collective-permute-done((f32[169,128]{1,0:T(8,128)S(1)}, f32[169,128]{1,0:T(8,128)S(1)}, u32[]{:S(2)}, u32[]{:S(2)}) %collective-permute-start.1) | collective-permute-done | bytes 86560 | tf_op jit(solution)/shard_map/ppermute | solution.py:26
  43.7 4.4 %gather_fusion.4 = bf16[1372,128]{1,0:T(8,128)(2,1)} fusion(bf16[937,128]{1,0:T(8,128)(2,1)S(1)} %pad_maximum_fusion.1, s32[2048]{0:T(1024)} %copy-done.7), kind=kCustom, calls=%fused_computation.8.clone | custom fusion | bytes 707952 | tf_op jit(solution)/shard_map/jit(_take)/gather | solution.py:70
  49.9 2.4 convolution_bitcast_fusion.3
  52.4 2.1 reshape.529
  54.4 9.9 %scatter_custom_fusion.2 = f32[937,128]{1,0:T(8,128)} fusion(s32[1372]{0:T(1024)} %copy-done.25, f32[1372,128]{1,0:T(8,128)} %reshape.529, f32[]{:T(128)} %constant.234.clone.1), kind=kCustom, calls=%fused_computation.70 | custom fusion | flops 175616 | bytes 480256 | tf_op jit(solution)/shard_map/scatter-add | solution.py:76
  68.1 3.4 %collective-permute-done.3 = f32[169,128]{1,0:T(8,128)S(1)} collective-permute-done((f32[169,128]{1,0:T(8,128)S(1)}, f32[169,128]{1,0:T(8,128)S(1)}, u32[]{:S(2)}, u32[]{:S(2)}) %collective-permute-start.3) | collective-permute-done | bytes 86560 | tf_op jit(solution)/shard_map/ppermute | solution.py:26
  79.1 4.0 %gather_fusion.6 = bf16[1372,128]{1,0:T(8,128)(2,1)} fusion(bf16[937,128]{1,0:T(8,128)(2,1)S(1)} %pad_maximum_fusion.2, s32[2048]{0:T(1024)S(1)} %copy-done.8), kind=kCustom, calls=%fused_computation.9.clone | custom fusion | bytes 707952 | tf_op jit(solution)/shard_map/jit(_take)/gather | solution.py:70
  87.6 9.9 %scatter_custom_fusion.4 = f32[937,128]{1,0:T(8,128)} fusion(s32[1372]{0:T(1024)} %copy-done.25, f32[1372,128]{1,0:T(8,128)} %reshape.545, f32[]{:T(128)} %constant.234.clone.1), kind=kCustom, calls=%fused_computation.68 | custom fusion | flops 175616 | bytes 480256 | tf_op jit(solution)/shard_map/scatter-add | solution.py:76
  100.7 4.0 %collective-permute-done.5 = f32[169,128]{1,0:T(8,128)S(1)} collective-permute-done((f32[169,128]{1,0:T(8,128)S(1)}, f32[169,128]{1,0:T(8,128)S(1)}, u32[]{:S(2)}, u32[]{:S(2)}) %collective-permute-start.5) | collective-permute-done | bytes 86560 | tf_op jit(solution)/shard_map/ppermute | solution.py:26
  109.8 8.2 %all-gather.1 = f32[4,1,768]{2,1,0:T(1,128)S(1)} all-gather(f32[1,1,768]{2,1,0:T(1,128)S(1)} %convolution_bitcast_fusion.5), channel_id=2, replica_groups=mesh['band'=4,'domain'=8] {'band'}, dimensions={0}, use_global_device_ids=true | all-gather | bytes 15360 | tf_op jit(solution)/shard_map/all_gather | solution.py:18
  119.4 3.3 %all-to-all-start = ((f32[8,1,96]{2,1,0:T(1,128)}), f32[8,1,96]{2,1,0:T(1,128)S(1)}, u32[]{:S(2)}, u32[]{:S(2)}) async-start(f32[8,1,96]{2,1,0:T(1,128)} %bitcast.12), calls=%async_computation | async-start | bytes 8192 | tf_op jit(solution)/shard_map/all_to_all | solution.py:95
  122.7 5.4 %all-to-all-done = f32[8,1,96]{2,1,0:T(1,128)S(1)} async-done(((f32[8,1,96]{2,1,0:T(1,128)}), f32[8,1,96]{2,1,0:T(1,128)S(1)}, u32[]{:S(2)}, u32[]{:S(2)}) %all-to-all-start) | async-done | bytes 3104 | tf_op jit(solution)/shard_map/all_to_all | solution.py:95
  132.7 5.6 %gather_fusion.10 = f32[1458]{0:T(1024)S(1)} fusion(f32[849]{0:T(1024)S(1)} %pad_maximum_fusion.5, s32[2048]{0:T(1024)S(1)} %pad_clamp_fusion), kind=kCustom, calls=%fused_computation.3.clone | custom fusion | bytes 17496 | tf_op jit(solution)/shard_map/jit(_take)/gather | solution.py:81
  140.5 11.0 %scatter_custom_fusion.9 = f32[849]{0:T(1024)S(1)} fusion(s32[1458]{0:T(1024)S(1)} %fusion.46, f32[1458]{0:T(1024)S(1)} %reshape.585, f32[]{:T(128)} %constant.234.clone.1), kind=kCustom, calls=%fused_computation.137 | custom fusion | flops 1458 | bytes 3400 | tf_op jit(solution)/shard_map/scatter-add | solution.py:90
  154.0 3.3 %collective-permute-done.9 = f32[81]{0:T(128)S(1)} collective-permute-done((f32[81]{0:T(128)S(1)}, f32[81]{0:T(128)S(1)}, u32[]{:S(2)}, u32[]{:S(2)}) %collective-permute-start.9) | collective-permute-done | bytes 356 | tf_op jit(solution)/shard_map/ppermute | solution.py:26
  160.2 5.7 %gather_fusion.12 = f32[1458]{0:T(1024)S(1)} fusion(f32[849]{0:T(1024)S(1)} %pad_maximum_fusion.6, s32[2048]{0:T(1024)S(1)} %pad_clamp_fusion), kind=kCustom, calls=%fused_computation.13.clone | custom fusion | bytes 17496 | tf_op jit(solution)/shard_map/jit(_take)/gather | solution.py:81
  168.0 11.0 %scatter_custom_fusion.11 = f32[849]{0:T(1024)S(1)} fusion(s32[1458]{0:T(1024)S(1)} %fusion.46, f32[1458]{0:T(1024)S(1)} %reshape.601, f32[]{:T(128)} %constant.234.clone.1), kind=kCustom, calls=%fused_computation.135 | custom fusion | flops 1458 | bytes 3400 | tf_op jit(solution)/shard_map/scatter-add | solution.py:90
  180.1 4.7 %collective-permute-done.11 = f32[81]{0:T(128)S(1)} collective-permute-done((f32[81]{0:T(128)S(1)}, f32[81]{0:T(128)S(1)}, u32[]{:S(2)}, u32[]{:S(2)}) %collective-permute-start.11) | collective-permute-done | bytes 356 | tf_op jit(solution)/shard_map/ppermute | solution.py:26
  185.6 3.3 %all-to-all-start.1 = ((f32[8,1,96]{2,1,0:T(1,128)}), f32[8,1,96]{2,1,0:T(1,128)S(1)}, u32[]{:S(2)}, u32[]{:S(2)}) async-start(f32[8,1,96]{2,1,0:T(1,128)} %all_to_all.16), calls=%async_computation.1 | async-start | bytes 8192 | tf_op jit(solution)/shard_map/all_to_all | solution.py:95
  188.9 3.5 %collective-permute-start.6 = (bf16[169,128]{1,0:T(8,128)(2,1)S(1)}, bf16[169,128]{1,0:T(8,128)(2,1)S(1)}, u32[]{:S(2)}, u32[]{:S(2)}) collective-permute-start(bf16[169,128]{1,0:T(8,128)(2,1)S(1)} %slice.263), channel_id=1, source_target_pairs={{0,7},{1,0},{2,1},{3,2},{4,3},{5,4},{6,5},{7,6},{8,15},{9,8},{10,9... | collective-permute-start | bytes 129800 | tf_op jit(solution)/shard_map/ppermute | solution.py:26
  195.9 4.0 %gather_fusion.8 = bf16[1372,128]{1,0:T(8,128)(2,1)} fusion(bf16[937,128]{1,0:T(8,128)(2,1)S(1)} %pad_maximum_fusion.3, s32[2048]{0:T(1024)S(1)} %copy-done.8), kind=kCustom, calls=%fused_computation.10.clone | custom fusion | bytes 707952 | tf_op jit(solution)/shard_map/jit(_take)/gather | solution.py:70
  204.5 9.3 %scatter_custom_fusion.6 = f32[937,128]{1,0:T(8,128)S(1)} fusion(s32[1372]{0:T(1024)} %copy-done.25, f32[1372,128]{1,0:T(8,128)} %reshape.561, f32[]{:T(128)} %constant.234.clone.1), kind=kCustom, calls=%fused_computation.66 | custom fusion | flops 175616 | bytes 480256 | tf_op jit(solution)/shard_map/scatter-add | solution.py:76
  217.1 4.3 %collective-permute-done.7 = f32[169,128]{1,0:T(8,128)S(1)} collective-permute-done((f32[169,128]{1,0:T(8,128)}, f32[169,128]{1,0:T(8,128)S(1)}, u32[]{:S(2)}, u32[]{:S(2)}) %collective-permute-start.7) | collective-permute-done | bytes 86560 | tf_op jit(solution)/shard_map/ppermute | solution.py:26
  227.5 4.4 %gather_fusion.14 = bf16[1372,128]{1,0:T(8,128)(2,1)} fusion(bf16[937,128]{1,0:T(8,128)(2,1)S(1)} %pad_maximum_fusion.4, s32[2048]{0:T(1024)} %copy-done.7), kind=kCustom, calls=%fused_computation.11.clone | custom fusion | bytes 707952 | tf_op jit(solution)/shard_map/jit(_take)/gather | solution.py:70
  233.7 2.4 convolution_bitcast_fusion
  236.0 2.0 reshape.617
  238.0 9.9 %scatter_custom_fusion.13 = f32[937,128]{1,0:T(8,128)} fusion(s32[1372]{0:T(1024)} %copy-done.25, f32[1372,128]{1,0:T(8,128)} %reshape.617, f32[]{:T(128)} %constant.234.clone.1), kind=kCustom, calls=%fused_computation.64 | custom fusion | flops 175616 | bytes 480256 | tf_op jit(solution)/shard_map/scatter-add | solution.py:76
  251.1 4.0 %collective-permute-done.13 = f32[169,128]{1,0:T(8,128)S(1)} collective-permute-done((f32[169,128]{1,0:T(8,128)S(1)}, f32[169,128]{1,0:T(8,128)S(1)}, u32[]{:S(2)}, u32[]{:S(2)}) %collective-permute-start.13) | collective-permute-done | bytes 86560 | tf_op jit(solution)/shard_map/ppermute | solution.py:26
  257.6 2.0 multiply_subtract_fusion
  (199 shorter events, 88.9 us)
Async XLA Ops:
  0.6 137.8 %copy-start = (f32[729,729]{1,0:T(8,128)S(1)}, f32[729,729]{1,0:T(8,128)}, u32[]{:S(2)}) copy-start(f32[729,729]{1,0:T(8,128)} %param.39) | copy-start | bytes 6377296
  1.8 10.3 %collective-permute-start = (bf16[169,128]{1,0:T(8,128)(2,1)S(1)}, bf16[169,128]{1,0:T(8,128)(2,1)S(1)}, u32[]{:S(2)}, u32[]{:S(2)}) collective-permute-start(bf16[169,128]{1,0:T(8,128)(2,1)S(1)} %slice.251), channel_id=1, source_target_pairs={{0,7},{1,0},{2,1},{3,2},{4,3},{5,4},{6,5},{7,6},{8,15},{9,8},{10,9... | collective-permute-start | bytes 129800 | tf_op jit(solution)/shard_map/ppermute | solution.py:26
  16.5 22.1 %copy-start.2 = (f32[768,128]{1,0:T(8,128)S(1)}, f32[768,128]{1,0:T(8,128)}, u32[]{:S(2)}) copy-start(f32[768,128]{1,0:T(8,128)} %param.33) | copy-start | bytes 1179652
  31.2 5.8 %collective-permute-start.1 = (f32[169,128]{1,0:T(8,128)S(1)}, f32[169,128]{1,0:T(8,128)S(1)}, u32[]{:S(2)}, u32[]{:S(2)}) collective-permute-start(f32[169,128]{1,0:T(8,128)S(1)} %scatter_custom_fusion.1), channel_id=1, source_target_pairs={{0,1},{1,2},{2,3},{3,4},{4,5},{5,6},{6,7},{7,0},{8,9},{9,10},{10,1... | collective-permute-start | bytes 259592 | tf_op jit(solution)/shard_map/ppermute | solution.py:26
  39.5 1.8 collective-permute-start.2
  49.9 24.1 %copy-start.4 = (f32[768,128]{1,0:T(8,128)S(1)}, f32[768,128]{1,0:T(8,128)}, u32[]{:S(2)}) copy-start(f32[768,128]{1,0:T(8,128)} %copy-done.3) | copy-start | bytes 1179652
  49.9 24.1 %copy-start.10 = (f32[768]{0:T(1024)S(1)}, f32[768]{0:T(1024)}, u32[]{:S(2)}) copy-start(f32[768]{0:T(1024)} %param.34) | copy-start | bytes 9220
  49.9 24.1 %copy-start.14 = (f32[768]{0:T(1024)S(1)}, f32[768]{0:T(1024)}, u32[]{:S(2)}) copy-start(f32[768]{0:T(1024)} %broadcast_multiply_fusion.2) | copy-start | bytes 9220
  52.4 23.3 %copy-start.30 = (s32[1,8]{1,0:T(1,128)S(1)}, s32[1,8]{1,0:T(1,128)}, u32[]{:S(2)}) copy-start(s32[1,8]{1,0:T(1,128)} %param.43) | copy-start | bytes 100
  52.4 23.9 %copy-start.11 = (s32[2,729]{1,0:T(2,128)S(1)}, s32[2,729]{1,0:T(2,128)}, u32[]{:S(2)}) copy-start(s32[2,729]{1,0:T(2,128)} %param.40) | copy-start | bytes 17500
  52.4 24.0 %copy-start.17 = (s32[2,729]{1,0:T(2,128)S(1)}, s32[2,729]{1,0:T(2,128)}, u32[]{:S(2)}) copy-start(s32[2,729]{1,0:T(2,128)} %compare_select_fusion.2) | copy-start | bytes 17500
  54.4 24.6 %copy-start.8 = (s32[2048]{0:T(1024)S(1)}, s32[2048]{0:T(1024)}, u32[]{:S(2)}) copy-start(s32[2048]{0:T(1024)} %copy-done.7) | copy-start | bytes 24580
  65.7 5.8 %collective-permute-start.3 = (f32[169,128]{1,0:T(8,128)S(1)}, f32[169,128]{1,0:T(8,128)S(1)}, u32[]{:S(2)}, u32[]{:S(2)}) collective-permute-start(f32[169,128]{1,0:T(8,128)S(1)} %scatter_custom_fusion.3), channel_id=1, source_target_pairs={{0,1},{1,2},{2,3},{3,4},{4,5},{5,6},{6,7},{7,0},{8,9},{9,10},{10,1... | collective-permute-start | bytes 259592 | tf_op jit(solution)/shard_map/ppermute | solution.py:26
  75.3 2.1 collective-permute-start.4
  98.8 5.8 %collective-permute-start.5 = (f32[169,128]{1,0:T(8,128)S(1)}, f32[169,128]{1,0:T(8,128)S(1)}, u32[]{:S(2)}, u32[]{:S(2)}) collective-permute-start(f32[169,128]{1,0:T(8,128)S(1)} %scatter_custom_fusion.5), channel_id=1, source_target_pairs={{0,1},{1,2},{2,3},{3,4},{4,5},{5,6},{6,7},{7,0},{8,9},{9,10},{10,1... | collective-permute-start | bytes 259592 | tf_op jit(solution)/shard_map/ppermute | solution.py:26
  119.4 8.8 %all-to-all-start = ((f32[8,1,96]{2,1,0:T(1,128)}), f32[8,1,96]{2,1,0:T(1,128)S(1)}, u32[]{:S(2)}, u32[]{:S(2)}) async-start(f32[8,1,96]{2,1,0:T(1,128)} %bitcast.12), calls=%async_computation | async-start | bytes 8192 | tf_op jit(solution)/shard_map/all_to_all | solution.py:95
  129.4 1.3 collective-permute-start.8
  138.3 21.8 %copy-start.29 = (s32[1,81]{1,0:T(1,128)S(1)}, s32[1,81]{1,0:T(1,128)}, u32[]{:S(2)}) copy-start(s32[1,81]{1,0:T(1,128)} %param.41) | copy-start | bytes 976
  152.5 4.8 %collective-permute-start.9 = (f32[81]{0:T(128)S(1)}, f32[81]{0:T(128)S(1)}, u32[]{:S(2)}, u32[]{:S(2)}) collective-permute-start(f32[81]{0:T(128)S(1)} %scatter_custom_fusion.10), channel_id=1, source_target_pairs={{0,1},{1,2},{2,3},{3,4},{4,5},{5,6},{6,7},{7,0},{8,9},{9,10},{10,1... | collective-permute-start | bytes 980 | tf_op jit(solution)/shard_map/ppermute | solution.py:26
  157.3 1.6 collective-permute-start.10
  165.9 23.0 %copy-start.27 = (s32[8]{0:T(128)S(1)}, s32[8]{0:T(128)}, u32[]{:S(2)}) copy-start(s32[8]{0:T(128)} %fusion.60) | copy-start | bytes 100
  165.9 29.2 %copy-start.19 = (s32[1024]{0:T(1024)S(1)}, s32[1024]{0:T(1024)}, u32[]{:S(2)}) copy-start(s32[1024]{0:T(1024)} %copy-done.18) | copy-start | bytes 12292
  165.9 29.9 %copy-start.24 = (pred[169]{0:T(512)(128)(4,1)S(1)}, pred[169]{0:T(512)(128)(4,1)}, u32[]{:S(2)}) copy-start(pred[169]{0:T(512)(128)(4,1)} %copy-done.23) | copy-start | bytes 511
  180.0 4.8 %collective-permute-start.11 = (f32[81]{0:T(128)S(1)}, f32[81]{0:T(128)S(1)}, u32[]{:S(2)}, u32[]{:S(2)}) collective-permute-start(f32[81]{0:T(128)S(1)} %scatter_custom_fusion.12), channel_id=1, source_target_pairs={{0,1},{1,2},{2,3},{3,4},{4,5},{5,6},{6,7},{7,0},{8,9},{9,10},{10,1... | collective-permute-start | bytes 980 | tf_op jit(solution)/shard_map/ppermute | solution.py:26
  185.6 8.8 %all-to-all-start.1 = ((f32[8,1,96]{2,1,0:T(1,128)}), f32[8,1,96]{2,1,0:T(1,128)S(1)}, u32[]{:S(2)}, u32[]{:S(2)}) async-start(f32[8,1,96]{2,1,0:T(1,128)} %all_to_all.16), calls=%async_computation.1 | async-start | bytes 8192 | tf_op jit(solution)/shard_map/all_to_all | solution.py:95
  188.9 6.1 %collective-permute-start.6 = (bf16[169,128]{1,0:T(8,128)(2,1)S(1)}, bf16[169,128]{1,0:T(8,128)(2,1)S(1)}, u32[]{:S(2)}, u32[]{:S(2)}) collective-permute-start(bf16[169,128]{1,0:T(8,128)(2,1)S(1)} %slice.263), channel_id=1, source_target_pairs={{0,7},{1,0},{2,1},{3,2},{4,3},{5,4},{6,5},{7,6},{8,15},{9,8},{10,9... | collective-permute-start | bytes 129800 | tf_op jit(solution)/shard_map/ppermute | solution.py:26
  195.0 20.4 %copy-start.22 = (f32[768]{0:T(1024)}, f32[768]{0:T(1024)S(1)}, u32[]{:S(2)}) copy-start(f32[768]{0:T(1024)S(1)} %select_n.110) | copy-start | bytes 9220
  215.5 6.0 %collective-permute-start.7 = (f32[169,128]{1,0:T(8,128)}, f32[169,128]{1,0:T(8,128)S(1)}, u32[]{:S(2)}, u32[]{:S(2)}) collective-permute-start(f32[169,128]{1,0:T(8,128)} %scatter_custom_fusion.7), channel_id=1, source_target_pairs={{0,1},{1,2},{2,3},{3,4},{4,5},{5,6},{6,7},{7,0},{8,9},{9,10},{10,1... | collective-permute-start | bytes 259592 | tf_op jit(solution)/shard_map/ppermute | solution.py:26
  223.9 1.7 collective-permute-start.12
  233.7 24.0 %copy-start.16 = (f32[768]{0:T(1024)S(1)}, f32[768]{0:T(1024)}, u32[]{:S(2)}) copy-start(f32[768]{0:T(1024)} %copy-done.15) | copy-start | bytes 9220
  233.7 24.0 %copy-start.20 = (f32[768]{0:T(1024)S(1)}, f32[768]{0:T(1024)}, u32[]{:S(2)}) copy-start(f32[768]{0:T(1024)} %get-tuple-element.90) | copy-start | bytes 9220
  249.3 5.8 %collective-permute-start.13 = (f32[169,128]{1,0:T(8,128)S(1)}, f32[169,128]{1,0:T(8,128)S(1)}, u32[]{:S(2)}, u32[]{:S(2)}) collective-permute-start(f32[169,128]{1,0:T(8,128)S(1)} %scatter_custom_fusion.14), channel_id=1, source_target_pairs={{0,1},{1,2},{2,3},{3,4},{4,5},{5,6},{6,7},{7,0},{8,9},{9,10},{10,1... | collective-permute-start | bytes 259592 | tf_op jit(solution)/shard_map/ppermute | solution.py:26
  (16 other events, 143.2 us)
